TPU v7x, 256 devices: a whole 4x4x8 slice. The times are simulated.
256 devices in a mesh: seq: 128 (over z, y, x), head: 2 (over core).
Axes of the slice: x: 4, y: 4, z: 8, core: 2. Of those that a mesh axis runs over, the one named last changes fastest.
Arguments:
- input_rows: bfloat16 [32768, 4096], P(('seq', 'head')), may hold values from -40 to 40
- doc_lengths: int32 [64], replicated, may hold values from 1 to 1024, 32768 in all
- w_query: bfloat16 [4096, 4096], P(None, 'head'), may hold values from -0.09375 to 0.09375
- key_weight: bfloat16 [4096, 1024], P(None, 'head'), may hold values from -0.09375 to 0.09375
- value_weight: bfloat16 [4096, 1024], P(None, 'head'), may hold values from -0.09375 to 0.09375
- w_out: bfloat16 [4096, 4096], P('head'), may hold values from -0.5 to 0.5
Outputs:
- mixed: bfloat16 [32768, 4096], P(('seq', 'head'))
All inputs are finite; a program needn't handle non-finite values.
Results may differ from a plain program's by a relative error of at most 0.013.
Values may be sent and summed in bfloat16 or wider, within the bound.
A program may use at most 192 MiB of HBM per device.

v0:
```python
import math
import jax
import jax.numpy as jnp
from jax import lax
from jax.sharding import PartitionSpec as P

HEAD_SIZE = 128
REACH = 4
NEG_FILL = -1e30


def passed_along(value, axis, steps):
    count = lax.axis_size(axis)
    first, last = (max(0, -steps), min(count, count - steps))
    return lax.ppermute(value, axis, [(source, source + steps) for source in range(first, last)])


def inverse_frequency():
    table = []
    for number in range(HEAD_SIZE // 2):
        base_freq = 500000.0 ** (-(2.0 * number) / HEAD_SIZE)
        wavelength = 2.0 * math.pi / base_freq
        smooth = (8192.0 / wavelength - 1.0) / 3.0
        if wavelength < 2048.0:
            table.append(base_freq)
        elif wavelength > 8192.0:
            table.append(base_freq / 8.0)
        else:
            table.append((1.0 - smooth) * base_freq / 8.0 + smooth * base_freq)
    return jnp.asarray(table, dtype=jnp.float32)


def rotate(value_matrix, cosine, sine_table):
    half_size = value_matrix.shape[-1] // 2
    first = value_matrix[..., :half_size]
    second = value_matrix[..., half_size:]
    return jnp.concatenate(
        [first * cosine - second * sine_table, second * cosine + first * sine_table], axis=-1
    )


def doc_of(positions, doc_ends):
    return jnp.sum((positions[:, None] >= doc_ends[None, :]).astype(jnp.int32), axis=1)


def body(input_rows, doc_lengths, w_query, key_weight, value_weight, w_out):
    width_q = w_query.shape[1]
    width_k = key_weight.shape[1]
    heads_here = width_q // HEAD_SIZE
    kv_here = width_k // HEAD_SIZE
    query_group = heads_here // kv_here
    piece = lax.all_gather(input_rows, "head", axis=0, tiled=True)
    projected = jnp.concatenate(
        [
            jnp.dot(piece, w_query, preferred_element_type=jnp.float32),
            jnp.dot(piece, key_weight, preferred_element_type=jnp.float32),
            jnp.dot(piece, value_weight, preferred_element_type=jnp.float32),
        ],
        axis=1,
    )
    tok_seq = projected.shape[0]
    seq_index = lax.axis_index("seq")
    positions = seq_index * tok_seq + jnp.arange(tok_seq, dtype=jnp.int32)
    doc_ends = jnp.cumsum(doc_lengths)
    query_docs = doc_of(positions, doc_ends)
    angles = positions.astype(jnp.float32)[:, None] * inverse_frequency()[None, :]
    cosine = jnp.cos(angles)[:, None, :]
    sine_table = jnp.sin(angles)[:, None, :]
    query_matrix = rotate(
        projected[:, :width_q].reshape(tok_seq, heads_here, HEAD_SIZE), cosine, sine_table
    )
    query_matrix = query_matrix.astype(jnp.bfloat16).reshape(
        tok_seq, kv_here, query_group, HEAD_SIZE
    )
    key_matrix = rotate(
        projected[:, width_q : width_q + width_k].reshape(tok_seq, kv_here, HEAD_SIZE),
        cosine,
        sine_table,
    )
    key_matrix = key_matrix.astype(jnp.bfloat16).reshape(tok_seq, width_k)
    value_matrix = projected[:, width_q + width_k :].astype(jnp.bfloat16)
    scale = HEAD_SIZE ** (-0.5)

    def attend(state, key_rows, value_rows, key_pos):
        running_max, running_sum, weighted = state
        count = key_rows.shape[0]
        key_block = key_rows.reshape(count, kv_here, HEAD_SIZE)
        value_block = value_rows.reshape(count, kv_here, HEAD_SIZE)
        key_docs = doc_of(key_pos, doc_ends)
        scores = (
            jnp.einsum(
                "tkgd,skd->kgts", query_matrix, key_block, preferred_element_type=jnp.float32
            )
            * scale
        )
        allowed = (
            (query_docs[:, None] == key_docs[None, :])
            & (key_pos[None, :] <= positions[:, None])
            & (key_pos[None, :] >= 0)
        )
        scores = jnp.where(allowed, scores, NEG_FILL)
        new_max = jnp.maximum(running_max, jnp.max(scores, axis=-1))
        factor = jnp.exp(running_max - new_max)
        weights = jnp.where(allowed, jnp.exp(scores - new_max[..., None]), 0.0)
        running_sum = running_sum * factor + jnp.sum(weights, axis=-1)
        weighted = weighted * factor[..., None] + jnp.einsum(
            "kgts,skd->kgtd",
            weights.astype(jnp.bfloat16),
            value_block,
            preferred_element_type=jnp.float32,
        )
        return (new_max, running_sum, weighted)

    initial = (
        jnp.full((kv_here, query_group, tok_seq), NEG_FILL, jnp.float32),
        jnp.zeros((kv_here, query_group, tok_seq), jnp.float32),
        jnp.zeros((kv_here, query_group, tok_seq, HEAD_SIZE), jnp.float32),
    )
    state = attend(initial, key_matrix, value_matrix, positions)
    for distance in range(1, REACH + 1):
        earlier = passed_along((key_matrix, value_matrix), "seq", distance)
        state = attend(state, earlier[0], earlier[1], positions - distance * tok_seq)
    final_max, final_sum, final_weighted = state
    attended = (final_weighted / final_sum[..., None]).transpose(2, 0, 1, 3)
    attended = attended.reshape(tok_seq, heads_here * HEAD_SIZE).astype(jnp.bfloat16)
    return lax.psum_scatter(
        jnp.dot(attended, w_out, preferred_element_type=jnp.float32).astype(jnp.bfloat16),
        "head",
        scatter_dimension=0,
        tiled=True,
    )


def solution(mesh):
    in_specs = (
        P(("seq", "head"), None),
        P(),
        P(None, "head"),
        P(None, "head"),
        P(None, "head"),
        P("head", None),
    )
    out_specs = P(("seq", "head"), None)
    return jax.shard_map(body, mesh=mesh, in_specs=in_specs, out_specs=out_specs, check_vma=False)
```

profile of v0, /device:TPU:1, one launch (start us, length us, event | category | flops | bytes accessed | tf_op | source)
XLA Modules:
  0.0 153.8 jit_solution(9673739192024044991)
XLA Ops:
  6.5 0.7 all-gather.2.cloned.1.call-update
  7.3 0.7 copy.43
  8.5 1.2 multiply_cosine_fusion
  9.7 0.7 and_and_fusion.4
  10.4 19.2 %all-gather.2.cloned.1.call-done = bf16[256,4096]{1,0:T(8,128)(2,1)} async-done(((bf16[128,4096]{1,0:T(8,128)(2,1)}), bf16[256,4096]{1,0:T(8,128)(2,1)}) %all-gather.2.cloned.1.call-update) | async-done | bytes 2097168 | tf_op jit(solution)/shard_map/all_gather | solution.py:52
  29.6 4.1 %fusion.94 = f32[256,512]{1,0:T(8,128)S(1)} fusion(bf16[256,4096]{1,0:T(8,128)(2,1)} %all-gather.2.cloned.1.call-done, bf16[4096,512]{1,0:T(8,128)(2,1)} %param.10), kind=kOutput, calls=%fused_computation.140 | convolution fusion | flops 1073741824 | bytes 6815744 | tf_op jit(solution)/shard_map/dot_general | solution.py:56
  33.7 0.2 reshape.280
  33.9 0.3 fusion.93
  34.2 0.1 multiply_subtract_fusion
  34.4 0.1 maximum_convert_fusion
  34.5 0.1 copy.50
  34.7 4.4 %collective-permute-start.2 = (bf16[256,512]{0,1:T(8,128)(2,1)S(1)}, bf16[256,512]{0,1:T(8,128)(2,1)S(1)}, u32[]{:S(2)}, u32[]{:S(2)}) collective-permute-start(bf16[256,512]{0,1:T(8,128)(2,1)S(1)} %bitcast.274), channel_id=1, source_target_pairs={{0,4},{2,6},{4,8},{6,10},{8,12},{10,14},{12,16},{14,18},{16,20},{1... | collective-permute-start | bytes 786440 | tf_op jit(solution)/shard_map/ppermute | solution.py:15
  39.0 2.2 %collective-permute-start = (bf16[256,512]{0,1:T(8,128)(2,1)S(1)}, bf16[256,512]{0,1:T(8,128)(2,1)S(1)}, u32[]{:S(2)}, u32[]{:S(2)}) collective-permute-start(bf16[256,512]{0,1:T(8,128)(2,1)S(1)} %bitcast.275), channel_id=1, source_target_pairs={{0,2},{2,4},{4,6},{6,8},{8,10},{10,12},{12,14},{14,16},{16,18},{18... | collective-permute-start | bytes 786440 | tf_op jit(solution)/shard_map/ppermute | solution.py:15
  41.3 3.1 %collective-permute-start.6 = (bf16[256,512]{0,1:T(8,128)(2,1)S(1)}, bf16[256,512]{0,1:T(8,128)(2,1)S(1)}, u32[]{:S(2)}, u32[]{:S(2)}) collective-permute-start(bf16[256,512]{0,1:T(8,128)(2,1)S(1)} %bitcast.276), channel_id=1, source_target_pairs={{0,8},{2,10},{4,12},{6,14},{8,16},{10,18},{12,20},{14,22},{16,24},... | collective-permute-start | bytes 786440 | tf_op jit(solution)/shard_map/ppermute | solution.py:15
  44.4 5.2 %collective-permute-start.4 = (bf16[256,512]{0,1:T(8,128)(2,1)S(1)}, bf16[256,512]{0,1:T(8,128)(2,1)S(1)}, u32[]{:S(2)}, u32[]{:S(2)}) collective-permute-start(bf16[256,512]{0,1:T(8,128)(2,1)S(1)} %bitcast.277), channel_id=1, source_target_pairs={{0,6},{2,8},{4,10},{6,12},{8,14},{10,16},{12,18},{14,20},{16,22},{... | collective-permute-start | bytes 786440 | tf_op jit(solution)/shard_map/ppermute | solution.py:15
  49.6 4.1 %convolution_convert_fusion.1 = bf16[256,512]{1,0:T(8,128)(2,1)S(1)} fusion(bf16[256,4096]{1,0:T(8,128)(2,1)} %all-gather.2.cloned.1.call-done, bf16[4096,512]{1,0:T(8,128)(2,1)} %param.11), kind=kOutput, calls=%fused_computation.70 | convolution fusion | flops 1073872896 | bytes 6553600 | tf_op jit(solution)/shard_map/dot_general | solution.py:57
  53.7 0.1 copy.78
  53.8 1.3 collective-permute-start.1
  55.1 8.7 %convolution_bitcast_fusion = f32[32,8,16,128]{3,1,2,0:T(8,128)S(1)} fusion(bf16[256,4096]{1,0:T(8,128)(2,1)} %all-gather.2.cloned.1.call-done, bf16[4096,2048]{1,0:T(8,128)(2,1)} %param.9), kind=kOutput, calls=%fused_computation.69 | convolution fusion | flops 4294967296 | bytes 20971520 | tf_op jit(solution)/shard_map/dot_general | solution.py:55
  63.9 0.4 copy.93
  64.3 0.8 subtract_convert_fusion
  65.0 0.3 copy.46
  65.3 0.3 copy.47
  65.6 0.6 pad_maximum_fusion
  66.2 0.8 fusion
  67.0 4.0 %collective-permute-start.3 = (bf16[256,512]{1,0:T(8,128)(2,1)S(1)}, bf16[256,512]{1,0:T(8,128)(2,1)S(1)}, u32[]{:S(2)}, u32[]{:S(2)}) collective-permute-start(bf16[256,512]{1,0:T(8,128)(2,1)S(1)} %convolution_convert_fusion.1), channel_id=1, source_target_pairs={{0,4},{2,6},{4,8},{6,10},{8,12},{10,14},{12,16},{14,18},{16,20},{1... | collective-permute-start | bytes 786440 | tf_op jit(solution)/shard_map/ppermute | solution.py:15
  71.0 2.9 %fusion.2 = (f32[4,4,256]{2,1,0:T(4,128)S(1)}, f32[4,256,256,4]{2,1,3,0:T(8,128)}) fusion(pred[256,256]{0,1:T(8,128)(4,1)S(1)} %get-tuple-element.28, bf16[256,4,128,1]{0,2,3,1:T(8,128)(2,1)S(1)} %bitcast.272, bf16[256,4,4,128]{3,0,2,1:T(8,128)(2,1)S(1)} %pad_maximum_fusion), kind=kOutput, calls=%fused_computation.13 | convolution fusion | flops 271577088 | bytes 5586944 | tf_op jit(solution)/shard_map/tkgd,skd->kgts/dot_general | solution.py:91
  73.8 3.7 %collective-permute-start.5 = (bf16[256,512]{1,0:T(8,128)(2,1)S(1)}, bf16[256,512]{1,0:T(8,128)(2,1)S(1)}, u32[]{:S(2)}, u32[]{:S(2)}) collective-permute-start(bf16[256,512]{1,0:T(8,128)(2,1)S(1)} %convolution_convert_fusion.1), channel_id=1, source_target_pairs={{0,6},{2,8},{4,10},{6,12},{8,14},{10,16},{12,18},{14,20},{16,22},{... | collective-permute-start | bytes 786440 | tf_op jit(solution)/shard_map/ppermute | solution.py:15
  77.6 0.9 fusion.1
  78.5 3.3 %collective-permute-start.7 = (bf16[256,512]{1,0:T(8,128)(2,1)S(1)}, bf16[256,512]{1,0:T(8,128)(2,1)S(1)}, u32[]{:S(2)}, u32[]{:S(2)}) collective-permute-start(bf16[256,512]{1,0:T(8,128)(2,1)S(1)} %convolution_convert_fusion.1), channel_id=1, source_target_pairs={{0,8},{2,10},{4,12},{6,14},{8,16},{10,18},{12,20},{14,22},{16,24},... | collective-permute-start | bytes 786440 | tf_op jit(solution)/shard_map/ppermute | solution.py:15
  81.8 2.8 %fusion.4 = (f32[4,4,256]{2,1,0:T(4,128)S(1)}, f32[4,256,256,4]{2,1,3,0:T(8,128)}) fusion(pred[256,256]{0,1:T(8,128)(4,1)S(1)} %get-tuple-element.30, bf16[256,4,128,1]{0,2,3,1:T(8,128)(2,1)S(1)} %bitcast.270, bf16[256,4,4,128]{3,0,2,1:T(8,128)(2,1)S(1)} %pad_maximum_fusion), kind=kOutput, calls=%fused_computation.15 | convolution fusion | flops 271577088 | bytes 5586944 | tf_op jit(solution)/shard_map/tkgd,skd->kgts/dot_general | solution.py:91
  84.6 2.9 %fusion.3 = (f32[4,4,256]{2,1,0:T(4,128)S(1)}, f32[4,256,256,4]{2,1,3,0:T(8,128)}) fusion(pred[256,256]{0,1:T(8,128)(4,1)S(1)} %get-tuple-element.29, bf16[256,4,128,1]{0,2,3,1:T(8,128)(2,1)S(1)} %bitcast.269, bf16[256,4,4,128]{3,0,2,1:T(8,128)(2,1)S(1)} %pad_maximum_fusion), kind=kOutput, calls=%fused_computation.14 | convolution fusion | flops 271577088 | bytes 5586944 | tf_op jit(solution)/shard_map/tkgd,skd->kgts/dot_general | solution.py:91
  87.5 1.0 fusion.5
  88.5 2.5 %fusion.23 = f32[4,4,256,128]{2,3,1,0:T(8,128)} fusion(bf16[256,4,128,1]{0,2,3,1:T(8,128)(2,1)S(1)} %bitcast.273, f32[4,256,256,4]{2,1,3,0:T(8,128)S(1)} %get-tuple-element.43, f32[4,4,256]{2,1,0:T(4,128)S(1)} %get-tuple-element.26, pred[256,256]{0,1:T(8,128)(4,1)S(1)} %get-tuple-element.27), kind=kOutput, calls=%fused_computation.30 | convolution fusion | flops 273678336 | bytes 6635520 | tf_op jit(solution)/shard_map/kgts,skd->kgtd/dot_general | solution.py:106
  91.1 1.0 fusion.7
  92.1 0.1 copy.81
  92.3 4.9 %fusion.21 = f32[4,4,256,128]{2,3,1,0:T(8,128)} fusion(bf16[256,4,128,1]{0,2,3,1:T(8,128)(2,1)S(1)} %bitcast.279, f32[4,256,256,4]{2,1,3,0:T(8,128)} %copy-done.3, f32[4,4,256]{2,1,0:T(4,128)S(1)} %get-tuple-element.17, pred[256,256]{0,1:T(8,128)(4,1)S(1)} %get-tuple-element.31), kind=kOutput, calls=%fused_computation.29 | convolution fusion | flops 273678336 | bytes 6635520 | tf_op jit(solution)/shard_map/kgts,skd->kgtd/dot_general | solution.py:106
  97.2 1.0 fusion.9
  98.2 0.1 copy.84
  98.4 4.9 %fusion.19 = f32[4,4,256,128]{2,3,1,0:T(8,128)} fusion(bf16[256,4,128,1]{0,2,3,1:T(8,128)(2,1)S(1)} %bitcast.280, f32[4,256,256,4]{2,1,3,0:T(8,128)} %get-tuple-element.39, f32[4,4,256]{2,1,0:T(4,128)S(1)} %get-tuple-element.16, pred[256,256]{0,1:T(8,128)(4,1)S(1)} %get-tuple-element.28), kind=kOutput, calls=%fused_computation.28 | convolution fusion | flops 273678336 | bytes 6635520 | tf_op jit(solution)/shard_map/kgts,skd->kgtd/dot_general | solution.py:106
  103.3 1.0 fusion.11
  104.3 0.1 copy.87
  104.5 4.9 %fusion.17 = f32[4,4,256,128]{2,3,1,0:T(8,128)} fusion(bf16[256,4,128,1]{0,2,3,1:T(8,128)(2,1)S(1)} %bitcast.281, f32[4,256,256,4]{2,1,3,0:T(8,128)} %get-tuple-element.37, f32[4,4,256]{2,1,0:T(4,128)S(1)} %get-tuple-element.15, pred[256,256]{0,1:T(8,128)(4,1)S(1)} %get-tuple-element.29), kind=kOutput, calls=%fused_computation.27 | convolution fusion | flops 273678336 | bytes 6635520 | tf_op jit(solution)/shard_map/kgts,skd->kgtd/dot_general | solution.py:106
  109.3 1.0 fusion.13
  110.4 0.1 copy.90
  110.6 6.6 %fusion.26 = bf16[256,4,4,128]{0,3,2,1:T(8,128)(2,1)S(1)} fusion(f32[4,4,256,128]{2,3,1,0:T(8,128)} %fusion.17, f32[4,4,256,128]{2,3,1,0:T(8,128)} %fusion.19, f32[4,4,256,128]{2,3,1,0:T(8,128)} %fusion.21, f32[4,4,256,128]{2,3,1,0:T(8,128)} %fusion.23, f32[256,4,4]{0,2,1:T(4,128)S(1)} %get-tuple-element.10, f32[256,4,4]{0,2,1:T(4,128)S(1)} %get-tuple-element.13, ...), kind=kOutput, calls=%fused_computation.33 | convolution fusion | flops 279445504 | bytes 14073856 | tf_op jit(solution)/shard_map/kgts,skd->kgtd/dot_general | solution.py:106
  117.2 11.6 %convolution_convert_fusion = bf16[256,4096]{1,0:T(8,128)(2,1)} fusion(bf16[256,2048]{0,1:T(8,128)(2,1)S(1)} %bitcast.268, bf16[2048,4096]{1,0:T(8,128)(2,1)} %param.12), kind=kOutput, calls=%fused_computation | convolution fusion | flops 4296015872 | bytes 19922944 | tf_op jit(solution)/shard_map/dot_general | solution.py:127
  128.8 18.1 %reduce-scatter.2.cloned.1.call-done = bf16[128,4096]{1,0:T(8,128)(2,1)} async-done(((bf16[256,4096]{1,0:T(8,128)(2,1)}), bf16[128,4096]{1,0:T(8,128)(2,1)}) %reduce-scatter.2.cloned.1.call-update) | async-done | bytes 1048592 | tf_op jit(solution)/shard_map/reduce_scatter | solution.py:126
  (30 shorter events, 0.5 us)
Async XLA Ops:
  6.5 23.1 %all-gather.2.cloned.1.call-start = ((), (), s32[]{:S(2)}) async-start(), calls=%async_computation.1 | async-start | bytes 3145728 | tf_op jit(solution)/shard_map/all_gather | solution.py:52
  7.3 139.7 %reduce-scatter.2.cloned.1.call-start = ((), (), s32[]{:S(2)}) async-start(), calls=%async_computation.2 | async-start | bytes 3145728 | tf_op jit(solution)/shard_map/reduce_scatter | solution.py:126
  34.7 32.3 %collective-permute-start.2 = (bf16[256,512]{0,1:T(8,128)(2,1)S(1)}, bf16[256,512]{0,1:T(8,128)(2,1)S(1)}, u32[]{:S(2)}, u32[]{:S(2)}) collective-permute-start(bf16[256,512]{0,1:T(8,128)(2,1)S(1)} %bitcast.274), channel_id=1, source_target_pairs={{0,4},{2,6},{4,8},{6,10},{8,12},{10,14},{12,16},{14,18},{16,20},{1... | collective-permute-start | bytes 786440 | tf_op jit(solution)/shard_map/ppermute | solution.py:15
  39.0 34.8 %collective-permute-start = (bf16[256,512]{0,1:T(8,128)(2,1)S(1)}, bf16[256,512]{0,1:T(8,128)(2,1)S(1)}, u32[]{:S(2)}, u32[]{:S(2)}) collective-permute-start(bf16[256,512]{0,1:T(8,128)(2,1)S(1)} %bitcast.275), channel_id=1, source_target_pairs={{0,2},{2,4},{4,6},{6,8},{8,10},{10,12},{12,14},{14,16},{16,18},{18... | collective-permute-start | bytes 786440 | tf_op jit(solution)/shard_map/ppermute | solution.py:15
  41.3 37.2 %collective-permute-start.6 = (bf16[256,512]{0,1:T(8,128)(2,1)S(1)}, bf16[256,512]{0,1:T(8,128)(2,1)S(1)}, u32[]{:S(2)}, u32[]{:S(2)}) collective-permute-start(bf16[256,512]{0,1:T(8,128)(2,1)S(1)} %bitcast.276), channel_id=1, source_target_pairs={{0,8},{2,10},{4,12},{6,14},{8,16},{10,18},{12,20},{14,22},{16,24},... | collective-permute-start | bytes 786440 | tf_op jit(solution)/shard_map/ppermute | solution.py:15
  44.4 40.2 %collective-permute-start.4 = (bf16[256,512]{0,1:T(8,128)(2,1)S(1)}, bf16[256,512]{0,1:T(8,128)(2,1)S(1)}, u32[]{:S(2)}, u32[]{:S(2)}) collective-permute-start(bf16[256,512]{0,1:T(8,128)(2,1)S(1)} %bitcast.277), channel_id=1, source_target_pairs={{0,6},{2,8},{4,10},{6,12},{8,14},{10,16},{12,18},{14,20},{16,22},{... | collective-permute-start | bytes 786440 | tf_op jit(solution)/shard_map/ppermute | solution.py:15
  53.8 38.3 %collective-permute-start.1 = (bf16[256,512]{1,0:T(8,128)(2,1)S(1)}, bf16[256,512]{1,0:T(8,128)(2,1)S(1)}, u32[]{:S(2)}, u32[]{:S(2)}) collective-permute-start(bf16[256,512]{1,0:T(8,128)(2,1)S(1)} %convolution_convert_fusion.1), channel_id=1, source_target_pairs={{0,2},{2,4},{4,6},{6,8},{8,10},{10,12},{12,14},{14,16},{16,18},{18... | collective-permute-start | bytes 786440 | tf_op jit(solution)/shard_map/ppermute | solution.py:15
  67.0 31.2 %collective-permute-start.3 = (bf16[256,512]{1,0:T(8,128)(2,1)S(1)}, bf16[256,512]{1,0:T(8,128)(2,1)S(1)}, u32[]{:S(2)}, u32[]{:S(2)}) collective-permute-start(bf16[256,512]{1,0:T(8,128)(2,1)S(1)} %convolution_convert_fusion.1), channel_id=1, source_target_pairs={{0,4},{2,6},{4,8},{6,10},{8,12},{10,14},{12,16},{14,18},{16,20},{1... | collective-permute-start | bytes 786440 | tf_op jit(solution)/shard_map/ppermute | solution.py:15
  73.8 30.5 %collective-permute-start.5 = (bf16[256,512]{1,0:T(8,128)(2,1)S(1)}, bf16[256,512]{1,0:T(8,128)(2,1)S(1)}, u32[]{:S(2)}, u32[]{:S(2)}) collective-permute-start(bf16[256,512]{1,0:T(8,128)(2,1)S(1)} %convolution_convert_fusion.1), channel_id=1, source_target_pairs={{0,6},{2,8},{4,10},{6,12},{8,14},{10,16},{12,18},{14,20},{16,22},{... | collective-permute-start | bytes 786440 | tf_op jit(solution)/shard_map/ppermute | solution.py:15
  78.5 12.6 %copy-start.3 = (f32[4,256,256,4]{2,1,3,0:T(8,128)}, f32[4,256,256,4]{2,1,3,0:T(8,128)S(1)}, u32[]{:S(2)}) copy-start(f32[4,256,256,4]{2,1,3,0:T(8,128)S(1)} %get-tuple-element.41) | copy-start | bytes 12582916
  78.5 31.9 %collective-permute-start.7 = (bf16[256,512]{1,0:T(8,128)(2,1)S(1)}, bf16[256,512]{1,0:T(8,128)(2,1)S(1)}, u32[]{:S(2)}, u32[]{:S(2)}) collective-permute-start(bf16[256,512]{1,0:T(8,128)(2,1)S(1)} %convolution_convert_fusion.1), channel_id=1, source_target_pairs={{0,8},{2,10},{4,12},{6,14},{8,16},{10,18},{12,20},{14,22},{16,24},... | collective-permute-start | bytes 786440 | tf_op jit(solution)/shard_map/ppermute | solution.py:15
  92.3 4.9 %copy-start.1 = (f32[4,256,256,4]{2,1,3,0:T(8,128)S(1)}, f32[4,256,256,4]{2,1,3,0:T(8,128)}, u32[]{:S(2)}) copy-start(f32[4,256,256,4]{2,1,3,0:T(8,128)} %get-tuple-element.39) | copy-start | bytes 12582916
  98.4 4.9 %copy-start.2 = (f32[4,256,256,4]{2,1,3,0:T(8,128)S(1)}, f32[4,256,256,4]{2,1,3,0:T(8,128)}, u32[]{:S(2)}) copy-start(f32[4,256,256,4]{2,1,3,0:T(8,128)} %get-tuple-element.37) | copy-start | bytes 12582916
  104.5 4.9 %copy-start = (f32[4,256,256,4]{2,1,3,0:T(8,128)S(1)}, f32[4,256,256,4]{2,1,3,0:T(8,128)}, u32[]{:S(2)}) copy-start(f32[4,256,256,4]{2,1,3,0:T(8,128)} %get-tuple-element.35) | copy-start | bytes 12582916
Sparse Core Ops, SparseCore 0:
  9.2 20.4 all-gather.1
  128.9 17.9 reduce-scatter.1
where the time goes:
time: 154 us
  matrix products  62.4 us (41%)
  waiting for transfers between devices  38.1 us (25%)
  starting transfers between devices  27.3 us (18%)
  between operations  13.8 us (9%)
  other arithmetic  9.22 us (6%)
  local copies, waits for them, and re-layouts  3.01 us (2%)
    ppermute x8, starting transfers between devices, passed_along(): lax.ppermute(value, axis, [(source, source + steps) for source in range(f...  27.2 us
    dot_general x5, matrix products, attend(): jnp.einsum('kgts,skd->kgtd', weights.astype(jnp.bfloat16), value_block, p...  23.8 us
    all_gather x1, waiting for transfers between devices, body(): piece = lax.all_gather(input_rows, 'head', axis=0, tiled=True)  19.2 us
    reduce_scatter x1, waiting for transfers between devices, body(): lax.psum_scatter(jnp.dot(attended, w_out, preferred_element_type=jnp.floa...  18.1 us
    dot_general x1, matrix products, body(): jnp.dot(attended, w_out, preferred_element_type=jnp.float32)  11.6 us
    dot_general x5, matrix products, attend(): jnp.einsum('tkgd,skd->kgts', query_matrix, key_block, preferred_element_t...  10.2 us
    dot_general x1, matrix products, body(): jnp.dot(piece, w_query, preferred_element_type=jnp.float32)  8.73 us
    reduce_sum x5, other arithmetic, attend(): running_sum = running_sum * factor + jnp.sum(weights, axis=-1)  5.24 us
  transfers between devices with their start and end apart: 10, of which 2 were waited for; matrix products, arithmetic and copies ran while one was open for 33% of the time, Pallas kernels for 0%

commit v1 on v0

--- a/solution.py
+++ b/solution.py
@@ -49,7 +49,13 @@
     heads_here = width_q // HEAD_SIZE
     kv_here = width_k // HEAD_SIZE
     query_group = heads_here // kv_here
-    piece = lax.all_gather(input_rows, "head", axis=0, tiled=True)
+    plan_words = lambda load, d_out, axis_key: jnp.concatenate(
+        lax.all_to_all(
+            jnp.stack(lax.axis_size(axis_key) * [load]), axis_key, concat_axis=0, split_axis=0
+        ),
+        axis=d_out,
+    )
+    piece = plan_words(input_rows, 0, "head")
     projected = jnp.concatenate(
         [
             jnp.dot(piece, w_query, preferred_element_type=jnp.float32),

time: 154 us -> 175 us (1.14)
  local copies, waits for them, and re-layouts: 3.01 us -> 31.5 us
  waiting for transfers between devices: 38.1 us -> 19.1 us
  starting transfers between devices: 27.3 us -> 33.3 us
  other arithmetic: 9.22 us -> 14.2 us
    dot_general x0 -> x2, local copies, waits for them, and re-layouts: none -> 27.2 us  [the longest x1 20.7 us: body(): jnp.dot(piece, w_query, preferred_element_type=jnp.float32)]
    all_gather x1 -> x0, waiting for transfers between devices: 19.2 us -> none  [body(): piece = lax.all_gather(input_rows, 'head', axis=0, tiled=True)]
    all_to_all x0 -> x1, starting transfers between devices: none -> 6.99 us  [body(): lax.all_to_all(jnp.stack(lax.axis_size(axis_key) * [load]), axis_key, con...]
    another operation x3 -> x4, other arithmetic: 0.97 us -> 4.12 us  [the longest x1 3.06 us: body(): jnp.stack(lax.axis_size(axis_key) * [load])]
    reshape x5, local copies, waits for them, and re-layouts: 0.66 us -> 3.28 us  [attend(): value_block = value_rows.reshape(count, kv_here, HEAD_SIZE)]
    dot_general x1, matrix products: 4.06 us -> 2.01 us  [body(): jnp.dot(piece, value_weight, preferred_element_type=jnp.float32)]
    dot_general x5, matrix products: 10.2 us -> 12.2 us  [attend(): jnp.einsum('tkgd,skd->kgts', query_matrix, key_block, preferred_element_t...]
  transfers between devices with their start and end apart: 10 -> 10, of which waited for: 2 -> 1; matrix products, arithmetic and copies ran while one was open for 33% -> 47% of each run, Pallas kernels for 0% -> 0%
where the time goes in v1:
time: 175 us; the launch traced here: 173 us
  matrix products  61.3 us (35%)
  starting transfers between devices  33.3 us (19%)
  local copies, waits for them, and re-layouts  31.5 us (18%)
  waiting for transfers between devices  19.1 us (11%)
  other arithmetic  14.2 us (8%)
  between operations  13.8 us (8%)
    ppermute x8, starting transfers between devices, passed_along(): lax.ppermute(value, axis, [(source, source + steps) for source in range(f...  26.3 us
    dot_general x5, matrix products, attend(): jnp.einsum('kgts,skd->kgtd', weights.astype(jnp.bfloat16), value_block, p...  23.8 us
    dot_general x1, local copies, waits for them, and re-layouts, body(): jnp.dot(piece, w_query, preferred_element_type=jnp.float32)  20.7 us
    reduce_scatter x1, waiting for transfers between devices, body(): lax.psum_scatter(jnp.dot(attended, w_out, preferred_element_type=jnp.floa...  19.1 us
    dot_general x5, matrix products, attend(): jnp.einsum('tkgd,skd->kgts', query_matrix, key_block, preferred_element_t...  12.2 us
    dot_general x1, matrix products, body(): jnp.dot(attended, w_out, preferred_element_type=jnp.float32)  11.6 us
    dot_general x1, matrix products, body(): jnp.dot(piece, w_query, preferred_element_type=jnp.float32)  8.16 us
    all_to_all x1, starting transfers between devices, body(): lax.all_to_all(jnp.stack(lax.axis_size(axis_key) * [load]), axis_key, con...  6.99 us
  transfers between devices with their start and end apart: 10, of which 1 were waited for; matrix products, arithmetic and copies ran while one was open for 47% of the time, Pallas kernels for 0%

profile of v1, /device:TPU:1, one launch (start us, length us, event | category | flops | bytes accessed | tf_op | source)
XLA Modules:
  0.0 173.4 jit_solution(13545069527181864365)
XLA Ops:
  6.5 3.1 %pad_maximum_fusion = bf16[2,128,4096]{2,1,0:T(8,128)(2,1)} fusion(bf16[1,128,4096]{2,1,0:T(8,128)(2,1)} %bitcast.280), kind=kLoop, calls=%fused_computation.31 | loop fusion | flops 1048576 | bytes 3145728 | tf_op jit(solution)/shard_map/stack | solution.py:54
  9.6 7.0 %all-to-all-start = ((bf16[2,128,4096]{2,1,0:T(8,128)(2,1)}), bf16[2,128,4096]{2,1,0:T(8,128)(2,1)S(1)}, u32[]{:S(2)}, u32[]{:S(2)}) async-start(bf16[2,128,4096]{2,1,0:T(8,128)(2,1)} %pad_maximum_fusion), calls=%async_computation | async-start | bytes 4194304 | tf_op jit(solution)/shard_map/all_to_all | solution.py:53
  16.6 6.4 %copy.79 = bf16[512,4096]{1,0:T(8,128)(2,1)} copy(bf16[512,4096]{0,1:T(8,128)(2,1)} %bitcast.272) | data formatting | bytes 8388608 | tf_op jit(solution)/shard_map/dot_general | solution.py:62
  23.0 0.3 multiply_cosine_fusion
  23.4 3.6 %fusion.93 = f32[256,4,128]{0,2,1:T(8,128)S(1)} fusion(bf16[256,4096,1]{1,0,2:T(8,128)(2,1)S(1)} %bitcast.276, bf16[4,128,4096]{2,1,0:T(8,128)(2,1)} %bitcast.273), kind=kOutput, calls=%fused_computation.139 | convolution fusion | flops 1073741824 | bytes 6815744 | tf_op jit(solution)/shard_map/dot_general | solution.py:62
  27.1 0.7 maximum_convert_fusion
  27.8 2.2 %collective-permute-start = (bf16[256,512]{0,1:T(8,128)(2,1)}, bf16[256,512]{0,1:T(8,128)(2,1)}, u32[]{:S(2)}, u32[]{:S(2)}) collective-permute-start(bf16[256,512]{0,1:T(8,128)(2,1)} %bitcast.18), channel_id=1, source_target_pairs={{0,2},{2,4},{4,6},{6,8},{8,10},{10,12},{12,14},{14,16},{16,18},{18... | collective-permute-start | bytes 786440 | tf_op jit(solution)/shard_map/ppermute | solution.py:15
  30.0 4.4 %collective-permute-start.2 = (bf16[256,512]{0,1:T(8,128)(2,1)}, bf16[256,512]{0,1:T(8,128)(2,1)}, u32[]{:S(2)}, u32[]{:S(2)}) collective-permute-start(bf16[256,512]{0,1:T(8,128)(2,1)} %bitcast.18), channel_id=1, source_target_pairs={{0,4},{2,6},{4,8},{6,10},{8,12},{10,14},{12,16},{14,18},{16,20},{1... | collective-permute-start | bytes 786440 | tf_op jit(solution)/shard_map/ppermute | solution.py:15
  34.4 2.5 %collective-permute-start.6 = (bf16[256,512]{0,1:T(8,128)(2,1)}, bf16[256,512]{0,1:T(8,128)(2,1)S(1)}, u32[]{:S(2)}, u32[]{:S(2)}) collective-permute-start(bf16[256,512]{0,1:T(8,128)(2,1)} %bitcast.18), channel_id=1, source_target_pairs={{0,8},{2,10},{4,12},{6,14},{8,16},{10,18},{12,20},{14,22},{16,24},... | collective-permute-start | bytes 786440 | tf_op jit(solution)/shard_map/ppermute | solution.py:15
  36.9 4.1 %collective-permute-start.4 = (bf16[256,512]{0,1:T(8,128)(2,1)}, bf16[256,512]{0,1:T(8,128)(2,1)S(1)}, u32[]{:S(2)}, u32[]{:S(2)}) collective-permute-start(bf16[256,512]{0,1:T(8,128)(2,1)} %bitcast.18), channel_id=1, source_target_pairs={{0,6},{2,8},{4,10},{6,12},{8,14},{10,16},{12,18},{14,20},{16,22},{... | collective-permute-start | bytes 786440 | tf_op jit(solution)/shard_map/ppermute | solution.py:15
  41.0 2.0 %convolution_convert_fusion.1 = bf16[256,512]{1,0:T(8,128)(2,1)} fusion(bf16[256,4096]{1,0:T(8,128)(2,1)S(1)} %bitcast.277, bf16[4096,512]{1,0:T(8,128)(2,1)S(1)} %copy-done.14), kind=kOutput, calls=%fused_computation.68 | convolution fusion | flops 1073872896 | bytes 6553600 | tf_op jit(solution)/shard_map/dot_general | solution.py:63
  43.0 2.9 %collective-permute-start.1 = (bf16[256,512]{1,0:T(8,128)(2,1)}, bf16[256,512]{1,0:T(8,128)(2,1)}, u32[]{:S(2)}, u32[]{:S(2)}) collective-permute-start(bf16[256,512]{1,0:T(8,128)(2,1)} %convolution_convert_fusion.1), channel_id=1, source_target_pairs={{0,2},{2,4},{4,6},{6,8},{8,10},{10,12},{12,14},{14,16},{16,18},{18... | collective-permute-start | bytes 786440 | tf_op jit(solution)/shard_map/ppermute | solution.py:15
  45.9 0.6 fusion.69
  46.5 0.6 fusion.73
  47.1 0.6 broadcast_compare_fusion.1
  47.7 0.5 broadcast_compare_fusion.3
  48.2 1.8 %copy.83 = bf16[256,512]{0,1:T(8,128)(2,1)} copy(bf16[256,512]{1,0:T(8,128)(2,1)} %convolution_convert_fusion.1) | data formatting | bytes 524288 | tf_op jit(solution)/shard_map/reshape | solution.py:94
  50.2 0.6 reduce
  50.9 20.7 %copy.82 = bf16[2048,4096]{1,0:T(8,128)(2,1)} copy(bf16[2048,4096]{0,1:T(8,128)(2,1)} %bitcast.270) | data formatting | bytes 33554432 | tf_op jit(solution)/shard_map/dot_general | solution.py:61
  71.6 8.2 %fusion.94 = f32[256,16,128]{0,2,1:T(8,128)S(1)} fusion(bf16[256,4096,1]{1,0,2:T(8,128)(2,1)S(1)} %bitcast.278, bf16[16,128,4096]{2,1,0:T(8,128)(2,1)} %bitcast.271), kind=kOutput, calls=%fused_computation.140 | convolution fusion | flops 4294967296 | bytes 20971520 | tf_op jit(solution)/shard_map/dot_general | solution.py:61
  79.8 0.3 subtract_convert_fusion
  80.2 0.5 copy.47
  80.6 0.5 copy.48
  81.1 0.6 pad_maximum_fusion.1
  81.9 0.7 and_and_fusion.4
  82.6 0.9 fusion
  83.6 2.4 %collective-permute-start.3 = (bf16[256,512]{1,0:T(8,128)(2,1)}, bf16[256,512]{1,0:T(8,128)(2,1)S(1)}, u32[]{:S(2)}, u32[]{:S(2)}) collective-permute-start(bf16[256,512]{1,0:T(8,128)(2,1)} %convolution_convert_fusion.1), channel_id=1, source_target_pairs={{0,4},{2,6},{4,8},{6,10},{8,12},{10,14},{12,16},{14,18},{16,20},{1... | collective-permute-start | bytes 786440 | tf_op jit(solution)/shard_map/ppermute | solution.py:15
  86.0 1.8 %fusion.1 = (f32[4,4,256]{2,1,0:T(4,128)S(1)}, f32[4,256,256,4]{2,1,3,0:T(8,128)S(1)}) fusion(pred[256,256]{0,1:T(8,128)(4,1)S(1)} %get-tuple-element.29, bf16[256,4,128,1]{0,2,3,1:T(8,128)(2,1)} %bitcast.61, bf16[256,4,4,128]{3,0,2,1:T(8,128)(2,1)S(1)} %pad_maximum_fusion.1), kind=kOutput, calls=%fused_computation.12 | convolution fusion | flops 271577088 | bytes 5586944 | tf_op jit(solution)/shard_map/tkgd,skd->kgts/dot_general | solution.py:97
  87.9 4.4 %collective-permute-start.5 = (bf16[256,512]{1,0:T(8,128)(2,1)}, bf16[256,512]{1,0:T(8,128)(2,1)S(1)}, u32[]{:S(2)}, u32[]{:S(2)}) collective-permute-start(bf16[256,512]{1,0:T(8,128)(2,1)} %convolution_convert_fusion.1), channel_id=1, source_target_pairs={{0,6},{2,8},{4,10},{6,12},{8,14},{10,16},{12,18},{14,20},{16,22},{... | collective-permute-start | bytes 786440 | tf_op jit(solution)/shard_map/ppermute | solution.py:15
  92.3 3.8 %fusion.2 = (f32[4,4,256]{2,1,0:T(4,128)S(1)}, f32[4,256,256,4]{2,1,3,0:T(8,128)}) fusion(pred[256,256]{0,1:T(8,128)(4,1)S(1)} %get-tuple-element.26, bf16[256,4,128,1]{0,2,3,1:T(8,128)(2,1)} %bitcast.65, bf16[256,4,4,128]{3,0,2,1:T(8,128)(2,1)S(1)} %pad_maximum_fusion.1), kind=kOutput, calls=%fused_computation.13 | convolution fusion | flops 271577088 | bytes 5586944 | tf_op jit(solution)/shard_map/tkgd,skd->kgts/dot_general | solution.py:97
  96.1 3.4 %collective-permute-start.7 = (bf16[256,512]{1,0:T(8,128)(2,1)}, bf16[256,512]{1,0:T(8,128)(2,1)S(1)}, u32[]{:S(2)}, u32[]{:S(2)}) collective-permute-start(bf16[256,512]{1,0:T(8,128)(2,1)} %convolution_convert_fusion.1), channel_id=1, source_target_pairs={{0,8},{2,10},{4,12},{6,14},{8,16},{10,18},{12,20},{14,22},{16,24},... | collective-permute-start | bytes 786440 | tf_op jit(solution)/shard_map/ppermute | solution.py:15
  99.5 2.8 %fusion.4 = (f32[4,4,256]{2,1,0:T(4,128)S(1)}, f32[4,256,256,4]{2,1,3,0:T(8,128)}) fusion(pred[256,256]{0,1:T(8,128)(4,1)S(1)} %get-tuple-element.28, bf16[256,4,128,1]{0,2,3,1:T(8,128)(2,1)S(1)} %bitcast.282, bf16[256,4,4,128]{3,0,2,1:T(8,128)(2,1)S(1)} %pad_maximum_fusion.1), kind=kOutput, calls=%fused_computation.15 | convolution fusion | flops 271577088 | bytes 5586944 | tf_op jit(solution)/shard_map/tkgd,skd->kgts/dot_general | solution.py:97
  102.3 2.8 %fusion.3 = (f32[4,4,256]{2,1,0:T(4,128)S(1)}, f32[4,256,256,4]{2,1,3,0:T(8,128)}) fusion(pred[256,256]{0,1:T(8,128)(4,1)S(1)} %get-tuple-element.27, bf16[256,4,128,1]{0,2,3,1:T(8,128)(2,1)S(1)} %bitcast.281, bf16[256,4,4,128]{3,0,2,1:T(8,128)(2,1)S(1)} %pad_maximum_fusion.1), kind=kOutput, calls=%fused_computation.14 | convolution fusion | flops 271577088 | bytes 5586944 | tf_op jit(solution)/shard_map/tkgd,skd->kgts/dot_general | solution.py:97
  105.1 1.0 fusion.5
  106.2 2.6 %fusion.23 = f32[4,4,256,128]{2,3,1,0:T(8,128)} fusion(bf16[256,4,128,1]{0,2,3,1:T(8,128)(2,1)S(1)} %bitcast.283, f32[4,256,256,4]{2,1,3,0:T(8,128)S(1)} %get-tuple-element.41, f32[4,4,256]{2,1,0:T(4,128)S(1)} %get-tuple-element.24, pred[256,256]{0,1:T(8,128)(4,1)S(1)} %get-tuple-element.25), kind=kOutput, calls=%fused_computation.30 | convolution fusion | flops 273678336 | bytes 6635520 | tf_op jit(solution)/shard_map/kgts,skd->kgtd/dot_general | solution.py:112
  108.8 1.0 fusion.7
  109.9 1.1 copy.86
  111.0 4.8 %fusion.21 = f32[4,4,256,128]{2,3,1,0:T(8,128)} fusion(bf16[256,4,128,1]{0,2,3,1:T(8,128)(2,1)S(1)} %bitcast.285, f32[4,256,256,4]{2,1,3,0:T(8,128)} %copy-done.2, f32[4,4,256]{2,1,0:T(4,128)S(1)} %get-tuple-element.17, pred[256,256]{0,1:T(8,128)(4,1)S(1)} %get-tuple-element.29), kind=kOutput, calls=%fused_computation.29 | convolution fusion | flops 273678336 | bytes 6635520 | tf_op jit(solution)/shard_map/kgts,skd->kgtd/dot_general | solution.py:112
  115.8 1.0 fusion.9
  116.8 0.1 copy.89
  117.0 4.9 %fusion.19 = f32[4,4,256,128]{2,3,1,0:T(8,128)} fusion(bf16[256,4,128,1]{0,2,3,1:T(8,128)(2,1)S(1)} %bitcast.286, f32[4,256,256,4]{2,1,3,0:T(8,128)} %get-tuple-element.37, f32[4,4,256]{2,1,0:T(4,128)S(1)} %get-tuple-element.16, pred[256,256]{0,1:T(8,128)(4,1)S(1)} %get-tuple-element.26), kind=kOutput, calls=%fused_computation.28 | convolution fusion | flops 273678336 | bytes 6635520 | tf_op jit(solution)/shard_map/kgts,skd->kgtd/dot_general | solution.py:112
  121.9 1.0 fusion.11
  123.0 0.1 copy.92
  123.1 4.8 %fusion.17 = f32[4,4,256,128]{2,3,1,0:T(8,128)} fusion(bf16[256,4,128,1]{0,2,3,1:T(8,128)(2,1)S(1)} %bitcast.287, f32[4,256,256,4]{2,1,3,0:T(8,128)} %get-tuple-element.35, f32[4,4,256]{2,1,0:T(4,128)S(1)} %get-tuple-element.15, pred[256,256]{0,1:T(8,128)(4,1)S(1)} %get-tuple-element.27), kind=kOutput, calls=%fused_computation.27 | convolution fusion | flops 273678336 | bytes 6635520 | tf_op jit(solution)/shard_map/kgts,skd->kgtd/dot_general | solution.py:112
  127.9 1.0 fusion.13
  129.2 6.6 %fusion.26 = bf16[256,4,4,128]{0,3,2,1:T(8,128)(2,1)S(1)} fusion(f32[4,4,256,128]{2,3,1,0:T(8,128)} %fusion.17, f32[4,4,256,128]{2,3,1,0:T(8,128)} %fusion.19, f32[4,4,256,128]{2,3,1,0:T(8,128)} %fusion.21, f32[4,4,256,128]{2,3,1,0:T(8,128)} %fusion.23, f32[256,4,4]{0,2,1:T(4,128)S(1)} %get-tuple-element.10, f32[256,4,4]{0,2,1:T(4,128)S(1)} %get-tuple-element.13, ...), kind=kOutput, calls=%fused_computation.34 | convolution fusion | flops 279445504 | bytes 14073856 | tf_op jit(solution)/shard_map/kgts,skd->kgtd/dot_general | solution.py:112
  135.8 11.6 %convolution_convert_fusion = bf16[256,4096]{1,0:T(8,128)(2,1)} fusion(bf16[256,2048]{0,1:T(8,128)(2,1)S(1)} %bitcast.279, bf16[2048,4096]{1,0:T(8,128)(2,1)} %param.12), kind=kOutput, calls=%fused_computation | convolution fusion | flops 4296015872 | bytes 19922944 | tf_op jit(solution)/shard_map/dot_general | solution.py:133
  147.4 19.1 %reduce-scatter.2.cloned.1.call-done = bf16[128,4096]{1,0:T(8,128)(2,1)} async-done(((bf16[256,4096]{1,0:T(8,128)(2,1)}), bf16[128,4096]{1,0:T(8,128)(2,1)}) %reduce-scatter.2.cloned.1.call-update) | async-done | bytes 1048592 | tf_op jit(solution)/shard_map/reduce_scatter | solution.py:132
  (50 shorter events, 0.7 us)
Async XLA Ops:
  9.6 13.7 %all-to-all-start = ((bf16[2,128,4096]{2,1,0:T(8,128)(2,1)}), bf16[2,128,4096]{2,1,0:T(8,128)(2,1)S(1)}, u32[]{:S(2)}, u32[]{:S(2)}) async-start(bf16[2,128,4096]{2,1,0:T(8,128)(2,1)} %pad_maximum_fusion), calls=%async_computation | async-start | bytes 4194304 | tf_op jit(solution)/shard_map/all_to_all | solution.py:53
  16.6 149.9 %reduce-scatter.2.cloned.1.call-start = ((), (), s32[]{:S(2)}) async-start(), calls=%async_computation.2 | async-start | bytes 3145728 | tf_op jit(solution)/shard_map/reduce_scatter | solution.py:132
  16.6 6.4 %copy-start.13 = (f32[64]{0:T(128)S(1)}, f32[64]{0:T(128)}, u32[]{:S(2)}) copy-start(f32[64]{0:T(128)} %constant.39.clone) | copy-start | bytes 772
  23.3 17.6 %copy-start.14 = (bf16[4096,512]{1,0:T(8,128)(2,1)S(1)}, bf16[4096,512]{1,0:T(8,128)(2,1)}, u32[]{:S(2)}) copy-start(bf16[4096,512]{1,0:T(8,128)(2,1)} %param.11) | copy-start | bytes 12582916
  27.8 22.2 %copy-start.7 = (s32[64]{0:T(128)S(1)}, s32[64]{0:T(128)}, u32[]{:S(2)}) copy-start(s32[64]{0:T(128)} %param.8) | copy-start | bytes 772
  27.8 55.8 %collective-permute-start = (bf16[256,512]{0,1:T(8,128)(2,1)}, bf16[256,512]{0,1:T(8,128)(2,1)}, u32[]{:S(2)}, u32[]{:S(2)}) collective-permute-start(bf16[256,512]{0,1:T(8,128)(2,1)} %bitcast.18), channel_id=1, source_target_pairs={{0,2},{2,4},{4,6},{6,8},{8,10},{10,12},{12,14},{14,16},{16,18},{18... | collective-permute-start | bytes 786440 | tf_op jit(solution)/shard_map/ppermute | solution.py:15
  30.0 57.9 %collective-permute-start.2 = (bf16[256,512]{0,1:T(8,128)(2,1)}, bf16[256,512]{0,1:T(8,128)(2,1)}, u32[]{:S(2)}, u32[]{:S(2)}) collective-permute-start(bf16[256,512]{0,1:T(8,128)(2,1)} %bitcast.18), channel_id=1, source_target_pairs={{0,4},{2,6},{4,8},{6,10},{8,12},{10,14},{12,16},{14,18},{16,20},{1... | collective-permute-start | bytes 786440 | tf_op jit(solution)/shard_map/ppermute | solution.py:15
  34.4 61.7 %collective-permute-start.6 = (bf16[256,512]{0,1:T(8,128)(2,1)}, bf16[256,512]{0,1:T(8,128)(2,1)S(1)}, u32[]{:S(2)}, u32[]{:S(2)}) collective-permute-start(bf16[256,512]{0,1:T(8,128)(2,1)} %bitcast.18), channel_id=1, source_target_pairs={{0,8},{2,10},{4,12},{6,14},{8,16},{10,18},{12,20},{14,22},{16,24},... | collective-permute-start | bytes 786440 | tf_op jit(solution)/shard_map/ppermute | solution.py:15
  36.9 65.4 %collective-permute-start.4 = (bf16[256,512]{0,1:T(8,128)(2,1)}, bf16[256,512]{0,1:T(8,128)(2,1)S(1)}, u32[]{:S(2)}, u32[]{:S(2)}) collective-permute-start(bf16[256,512]{0,1:T(8,128)(2,1)} %bitcast.18), channel_id=1, source_target_pairs={{0,6},{2,8},{4,10},{6,12},{8,14},{10,16},{12,18},{14,20},{16,22},{... | collective-permute-start | bytes 786440 | tf_op jit(solution)/shard_map/ppermute | solution.py:15
  43.0 66.8 %collective-permute-start.1 = (bf16[256,512]{1,0:T(8,128)(2,1)}, bf16[256,512]{1,0:T(8,128)(2,1)}, u32[]{:S(2)}, u32[]{:S(2)}) collective-permute-start(bf16[256,512]{1,0:T(8,128)(2,1)} %convolution_convert_fusion.1), channel_id=1, source_target_pairs={{0,2},{2,4},{4,6},{6,8},{8,10},{10,12},{12,14},{14,16},{16,18},{18... | collective-permute-start | bytes 786440 | tf_op jit(solution)/shard_map/ppermute | solution.py:15
  80.1 1.6 copy-start.5
  80.1 1.6 copy-start.6
  80.1 1.8 %copy-start.8 = (pred[256]{0:T(512)(128)(4,1)S(1)}, pred[256]{0:T(512)(128)(4,1)}, u32[]{:S(2)}) copy-start(pred[256]{0:T(512)(128)(4,1)} %get-tuple-element.48) | copy-start | bytes 772
  80.1 1.7 %copy-start.9 = (pred[256]{0:T(512)(128)(4,1)S(1)}, pred[256]{0:T(512)(128)(4,1)}, u32[]{:S(2)}) copy-start(pred[256]{0:T(512)(128)(4,1)} %get-tuple-element.49) | copy-start | bytes 772
  80.1 1.7 %copy-start.10 = (pred[256]{0:T(512)(128)(4,1)S(1)}, pred[256]{0:T(512)(128)(4,1)}, u32[]{:S(2)}) copy-start(pred[256]{0:T(512)(128)(4,1)} %get-tuple-element.50) | copy-start | bytes 772
  80.1 1.7 %copy-start.11 = (pred[256]{0:T(512)(128)(4,1)S(1)}, pred[256]{0:T(512)(128)(4,1)}, u32[]{:S(2)}) copy-start(pred[256]{0:T(512)(128)(4,1)} %get-tuple-element.51) | copy-start | bytes 772
  80.1 1.7 %copy-start.12 = (pred[256]{0:T(512)(128)(4,1)S(1)}, pred[256]{0:T(512)(128)(4,1)}, u32[]{:S(2)}) copy-start(pred[256]{0:T(512)(128)(4,1)} %broadcast_compare_fusion.3) | copy-start | bytes 772
  83.6 33.3 %collective-permute-start.3 = (bf16[256,512]{1,0:T(8,128)(2,1)}, bf16[256,512]{1,0:T(8,128)(2,1)S(1)}, u32[]{:S(2)}, u32[]{:S(2)}) collective-permute-start(bf16[256,512]{1,0:T(8,128)(2,1)} %convolution_convert_fusion.1), channel_id=1, source_target_pairs={{0,4},{2,6},{4,8},{6,10},{8,12},{10,14},{12,16},{14,18},{16,20},{1... | collective-permute-start | bytes 786440 | tf_op jit(solution)/shard_map/ppermute | solution.py:15
  87.9 20.9 %copy-start.2 = (f32[4,256,256,4]{2,1,3,0:T(8,128)}, f32[4,256,256,4]{2,1,3,0:T(8,128)S(1)}, u32[]{:S(2)}) copy-start(f32[4,256,256,4]{2,1,3,0:T(8,128)S(1)} %get-tuple-element.39) | copy-start | bytes 12582916
  87.9 35.1 %collective-permute-start.5 = (bf16[256,512]{1,0:T(8,128)(2,1)}, bf16[256,512]{1,0:T(8,128)(2,1)S(1)}, u32[]{:S(2)}, u32[]{:S(2)}) collective-permute-start(bf16[256,512]{1,0:T(8,128)(2,1)} %convolution_convert_fusion.1), channel_id=1, source_target_pairs={{0,6},{2,8},{4,10},{6,12},{8,14},{10,16},{12,18},{14,20},{16,22},{... | collective-permute-start | bytes 786440 | tf_op jit(solution)/shard_map/ppermute | solution.py:15
  96.1 32.9 %collective-permute-start.7 = (bf16[256,512]{1,0:T(8,128)(2,1)}, bf16[256,512]{1,0:T(8,128)(2,1)S(1)}, u32[]{:S(2)}, u32[]{:S(2)}) collective-permute-start(bf16[256,512]{1,0:T(8,128)(2,1)} %convolution_convert_fusion.1), channel_id=1, source_target_pairs={{0,8},{2,10},{4,12},{6,14},{8,16},{10,18},{12,20},{14,22},{16,24},... | collective-permute-start | bytes 786440 | tf_op jit(solution)/shard_map/ppermute | solution.py:15
  102.3 3.9 %copy-start.4 = (bf16[256,512]{0,1:T(8,128)(2,1)S(1)}, bf16[256,512]{0,1:T(8,128)(2,1)}, u32[]{:S(2)}) copy-start(bf16[256,512]{0,1:T(8,128)(2,1)} %copy.83) | copy-start | bytes 786436
  110.9 4.8 %copy-start.1 = (f32[4,256,256,4]{2,1,3,0:T(8,128)S(1)}, f32[4,256,256,4]{2,1,3,0:T(8,128)}, u32[]{:S(2)}) copy-start(f32[4,256,256,4]{2,1,3,0:T(8,128)} %get-tuple-element.37) | copy-start | bytes 12582916
  117.0 4.9 %copy-start.3 = (f32[4,256,256,4]{2,1,3,0:T(8,128)S(1)}, f32[4,256,256,4]{2,1,3,0:T(8,128)}, u32[]{:S(2)}) copy-start(f32[4,256,256,4]{2,1,3,0:T(8,128)} %get-tuple-element.35) | copy-start | bytes 12582916
  123.1 4.8 %copy-start = (f32[4,256,256,4]{2,1,3,0:T(8,128)S(1)}, f32[4,256,256,4]{2,1,3,0:T(8,128)}, u32[]{:S(2)}) copy-start(f32[4,256,256,4]{2,1,3,0:T(8,128)} %get-tuple-element.33) | copy-start | bytes 12582916
Sparse Core Ops, SparseCore 0:
  147.5 18.9 reduce-scatter.1
